TPU v7x, 32 devices: a whole 2x2x4 slice. The times are simulated.
32 devices in a mesh: seq: 8 (over z, y), tok: 4 (over x, core).
Axes of the slice: x: 2, y: 2, z: 4, core: 2. Of those that a mesh axis runs over, the one named last changes fastest.
Arguments:
- tokens: bfloat16 [8, 1024, 1024], P('seq', 'tok'), may hold values from -6 to 6
- out_grad: bfloat16 [8, 1024, 1024], P('seq', 'tok'), may hold values from -6 to 6
- segments: int32 [8, 1024], P('seq'), may hold values from 0 to 2, never falling along the last dimension, each value on 1 to 512 neighbouring positions
- adapter_index: int32 [8], P('seq'), may hold values from 0 to 7
- qkv_weight: bfloat16 [1024, 3072], P('tok', 'seq'), may hold values from -0.1875 to 0.1875
- out_weight: bfloat16 [1024, 1024], P('tok', 'seq'), may hold values from -0.75 to 0.75
- in_weight: bfloat16 [1024, 5248], P('tok', 'seq'), may hold values from -0.1875 to 0.1875
- out2_weight: bfloat16 [2624, 1024], P('tok', 'seq'), may hold values from -0.15625 to 0.15625
- attn_gain: bfloat16 [1024], P('tok'), may hold values from 0.099609375 to 1.8984375
- mlp_gain: bfloat16 [1024], P('tok'), may hold values from 0.099609375 to 1.8984375
- qkv_down: bfloat16 [8, 16, 1024], replicated, may hold values from -0.1875 to 0.1875
- qkv_up: bfloat16 [8, 16, 3072], replicated, may hold values from -0.5 to 0.5
- out_down: bfloat16 [8, 16, 1024], replicated, may hold values from -0.1875 to 0.1875
- out_up: bfloat16 [8, 16, 1024], replicated, may hold values from -1.5 to 1.5
- in_down: bfloat16 [8, 16, 1024], replicated, may hold values from -0.1875 to 0.1875
- in_up: bfloat16 [8, 16, 5248], replicated, may hold values from -0.5 to 0.5
- out2_down: bfloat16 [8, 16, 2624], replicated, may hold values from -0.125 to 0.125
- out2_up: bfloat16 [8, 16, 1024], replicated, may hold values from -0.5 to 0.5
Outputs:
- layer_out: bfloat16 [8, 1024, 1024], P('seq', 'tok')
- input_grad: bfloat16 [8, 1024, 1024], P('seq', 'tok')
- qkv_down_grad: float32 [8, 16, 1024], replicated
- qkv_up_grad: float32 [8, 16, 3072], replicated
- out_down_grad: float32 [8, 16, 1024], replicated
- out_up_grad: float32 [8, 16, 1024], replicated
- in_down_grad: float32 [8, 16, 1024], replicated
- in_up_grad: float32 [8, 16, 5248], replicated
- out2_down_grad: float32 [8, 16, 2624], replicated
- out2_up_grad: float32 [8, 16, 1024], replicated
Inputs may be any that keep to these rules, and one draw needn't show every extreme that they name: `segments`: within a sequence the document numbers never fall; each document has 1 to 512 tokens, one of each sequence exactly 512.
All inputs are finite; a program needn't handle non-finite values.
Results may differ from a plain program's by a relative error of at most 0.018.
Values may be sent and summed in bfloat16 or wider, within the bound.
No kernel may reach another device: no remote copies, remote signals or barrier semaphores. Data moves between devices by JAX's collectives and lax.ppermute only.
A program may use at most 128 MiB of HBM per device.

v0:
```python
import jax
import jax.numpy as jnp
from jax import lax
from jax.sharding import PartitionSpec as P

HEADS = 16
HEAD_DIM = 64
FF = 2624
ADAPTERS = 8
EPS = 1e-05
THETA = 160000.0
HIGH = lax.Precision.HIGHEST


def layer_norm(values, gain_vec):
    middle = jnp.mean(values, axis=-1, keepdims=True)
    centered = values - middle
    spread = jnp.mean(centered * centered, axis=-1, keepdims=True)
    return centered * lax.rsqrt(spread + EPS) * gain_vec


def rotary_table(positions, head_width):
    exponent = jnp.arange(0, head_width, 2).astype(jnp.float32) / head_width
    inverse = 1.0 / THETA**exponent
    phases = positions.astype(jnp.float32)[:, None] * inverse[None, :]
    cosine = jnp.concatenate([jnp.cos(phases), jnp.cos(phases)], -1)
    sine_part = jnp.concatenate([jnp.sin(phases), jnp.sin(phases)], -1)
    return (cosine, sine_part)


def rotary(values, cosine, sine_part):
    half_width = values.shape[-1] // 2
    turned = jnp.concatenate([-values[..., half_width:], values[..., :half_width]], -1)
    return values * cosine[None, :, None, :] + turned * sine_part[None, :, None, :]


def glu_act(inputs, gate_vals):
    return jax.nn.gelu(inputs, approximate=False) * gate_vals


def select(table_rows, onehot_low):
    return jnp.einsum(
        "sa,ayz->syz", onehot_low, table_rows, preferred_element_type=jnp.float32
    ).astype(jnp.bfloat16)


def spread_back(term_rows, onehot):
    return jnp.einsum(
        "sa,syz->ayz", onehot, term_rows, precision=HIGH, preferred_element_type=jnp.float32
    )


def project(inputs, weight, down_rows, up_rows):
    seq_count, row_count, width_in = inputs.shape
    main_part = jnp.dot(
        inputs.reshape(seq_count * row_count, width_in), weight, preferred_element_type=jnp.float32
    )
    narrow = jnp.einsum(
        "std,srd->str", inputs, down_rows, preferred_element_type=jnp.float32
    ).astype(jnp.bfloat16)
    extra_part = jnp.einsum("str,sre->ste", narrow, up_rows, preferred_element_type=jnp.float32)
    return (main_part.reshape(seq_count, row_count, -1) + extra_part, narrow)


def project_back(grad_out, inputs, narrow, weight, down_rows, up_rows):
    seq_count, row_count, width_out = grad_out.shape
    main_part = lax.dot_general(
        grad_out.reshape(seq_count * row_count, width_out),
        weight,
        (((1,), (1,)), ((), ())),
        preferred_element_type=jnp.float32,
    )
    inner_grad = jnp.einsum(
        "ste,sre->str", grad_out, up_rows, preferred_element_type=jnp.float32
    ).astype(jnp.bfloat16)
    back_sum = main_part.reshape(seq_count, row_count, -1) + jnp.einsum(
        "str,srd->std", inner_grad, down_rows, preferred_element_type=jnp.float32
    )
    grad_up = jnp.einsum("str,ste->sre", narrow, grad_out, preferred_element_type=jnp.float32)
    grad_down = jnp.einsum("str,std->srd", inner_grad, inputs, preferred_element_type=jnp.float32)
    return (back_sum, grad_down, grad_up)


def masked_scores(query_part, key_part, doc_mask):
    scores = (
        jnp.einsum("sqhd,skhd->shqk", query_part, key_part, preferred_element_type=jnp.float32)
        * 0.125
    )
    return jnp.where(doc_mask[:, None, :, :], scores, -1e30)


def heads_slice(source, group_index, group_width, head_width):
    part_cols = lax.dynamic_slice_in_dim(source, group_index * group_width, group_width, 2)
    return part_cols.reshape(
        part_cols.shape[0], part_cols.shape[1], group_width // head_width, head_width
    )


def join_groups(parts):
    moved = jnp.moveaxis(parts, 0, 2)
    return moved.reshape(moved.shape[0], moved.shape[1], -1)


def body(
    tokens,
    out_grad,
    segments,
    adapter_index,
    qkv_weight,
    out_weight,
    in_weight,
    out2_weight,
    attn_gain,
    mlp_gain,
    qkv_down,
    qkv_up,
    out_down,
    out_up,
    in_down,
    in_up,
    out2_down,
    out2_up,
):
    seq_count, tok_rows, model_width = tokens.shape
    head_width = HEAD_DIM
    group_width = 2 * head_width
    groups = jnp.arange(HEADS // 2)
    seq_length = segments.shape[1]
    tok_start = lax.axis_index("tok") * tok_rows
    positions = tok_start + jnp.arange(tok_rows)
    cosine, sine_part = rotary_table(positions, head_width)
    own_segments = lax.dynamic_slice_in_dim(segments, tok_start, tok_rows, 1)
    doc_mask = own_segments[:, :, None] == segments[:, None, :]
    pick_bits = adapter_index[:, None] == jnp.arange(ADAPTERS)[None, :]
    onehot = pick_bits.astype(jnp.float32)
    onehot_low = pick_bits.astype(jnp.bfloat16)
    picked = [
        select(table_rows, onehot_low)
        for table_rows in (qkv_down, qkv_up, out_down, out_up, in_down, in_up, out2_down, out2_up)
    ]
    tok_parts = (
        lax.all_gather(qkv_weight, "tok", axis=0, tiled=True),
        lax.all_gather(out_weight, "tok", axis=0, tiled=True),
        lax.all_gather(in_weight, "tok", axis=0, tiled=True),
        lax.all_gather(out2_weight, "tok", axis=0, tiled=True),
        lax.all_gather(attn_gain, "tok", axis=0, tiled=True),
        lax.all_gather(mlp_gain, "tok", axis=0, tiled=True),
    )
    w_qkv, w_out, w_in, w_out2 = (
        lax.all_gather(tok_parts[0], "seq", axis=1, tiled=True),
        lax.all_gather(tok_parts[1], "seq", axis=1, tiled=True),
        lax.all_gather(tok_parts[2], "seq", axis=1, tiled=True),
        lax.all_gather(tok_parts[3], "seq", axis=1, tiled=True),
    )
    gain_one = tok_parts[4].astype(jnp.float32)
    gain_two = tok_parts[5].astype(jnp.float32)
    inputs = tokens.astype(jnp.float32)
    norm_one = layer_norm(inputs, gain_one).astype(jnp.bfloat16)
    qkv, narrow_qkv = project(norm_one, w_qkv, picked[0], picked[1])
    head_shape = (seq_count, tok_rows, HEADS, head_width)
    query_pre = qkv[..., :model_width].reshape(head_shape)
    query_low = (
        rotary(query_pre, cosine, sine_part)
        .reshape(seq_count, tok_rows, model_width)
        .astype(jnp.bfloat16)
    )
    key_low = (
        rotary(qkv[..., model_width : 2 * model_width].reshape(head_shape), cosine, sine_part)
        .reshape(seq_count, tok_rows, model_width)
        .astype(jnp.bfloat16)
    )
    value_low = qkv[..., 2 * model_width :].astype(jnp.bfloat16)
    keys_all, values_all = (
        lax.all_gather(key_low, "tok", axis=1, tiled=True),
        lax.all_gather(value_low, "tok", axis=1, tiled=True),
    )

    def forward_group(group_index):
        query_part = heads_slice(query_low, group_index, group_width, head_width)
        key_part = heads_slice(keys_all, group_index, group_width, head_width)
        value_part = heads_slice(values_all, group_index, group_width, head_width)
        scores = masked_scores(query_part, key_part, doc_mask)
        row_max = jnp.max(scores, axis=-1, keepdims=True)
        row_total = jnp.sum(jnp.exp(scores - row_max), axis=-1, keepdims=True)
        log_total = row_max + jnp.log(row_total)
        attn_prob = jnp.exp(scores - log_total).astype(jnp.bfloat16)
        mixed = jnp.einsum(
            "shqk,skhd->sqhd", attn_prob, value_part, preferred_element_type=jnp.float32
        )
        return (mixed.reshape(seq_count, tok_rows, group_width), log_total[..., 0])

    mixed_parts, log_totals = lax.map(forward_group, groups)
    attn_low = join_groups(mixed_parts).astype(jnp.bfloat16)
    attn_branch, narrow_out = project(attn_low, w_out, picked[2], picked[3])
    middle = inputs + attn_branch
    norm_two = layer_norm(middle, gain_two).astype(jnp.bfloat16)
    gate_up, narrow_in = project(norm_two, w_in, picked[4], picked[5])
    act_low = glu_act(gate_up[..., :FF], gate_up[..., FF:]).astype(jnp.bfloat16)
    mlp_branch, narrow_out2 = project(act_low, w_out2, picked[6], picked[7])
    layer_out = (middle + mlp_branch).astype(jnp.bfloat16)
    back_parts = (
        lax.all_gather(qkv_weight, "tok", axis=0, tiled=True),
        lax.all_gather(out_weight, "tok", axis=0, tiled=True),
        lax.all_gather(in_weight, "tok", axis=0, tiled=True),
        lax.all_gather(out2_weight, "tok", axis=0, tiled=True),
    )
    w_qkv, w_out, w_in, w_out2 = (
        lax.all_gather(back_parts[0], "seq", axis=1, tiled=True),
        lax.all_gather(back_parts[1], "seq", axis=1, tiled=True),
        lax.all_gather(back_parts[2], "seq", axis=1, tiled=True),
        lax.all_gather(back_parts[3], "seq", axis=1, tiled=True),
    )
    grad_y = out_grad.astype(jnp.float32)
    back_act, down_o2, up_o2 = project_back(
        out_grad, act_low, narrow_out2, w_out2, picked[6], picked[7]
    )
    _, glu_back = jax.vjp(glu_act, gate_up[..., :FF], gate_up[..., FF:])
    grad_in, grad_gate = glu_back(back_act)
    grad_z = jnp.concatenate([grad_in, grad_gate], axis=-1).astype(jnp.bfloat16)
    back_norm_two, down_in, up_in = project_back(
        grad_z, norm_two, narrow_in, w_in, picked[4], picked[5]
    )
    _, norm_two_back = jax.vjp(lambda field: layer_norm(field, gain_two), middle)
    grad_mid = grad_y + norm_two_back(back_norm_two)[0]
    grad_a = grad_mid.astype(jnp.bfloat16)
    back_attn, down_out, up_out = project_back(
        grad_a, attn_low, narrow_out, w_out, picked[2], picked[3]
    )
    grad_attn = back_attn.astype(jnp.bfloat16)

    def query_grads(group_index):
        query_part = heads_slice(query_low, group_index, group_width, head_width)
        key_part = heads_slice(keys_all, group_index, group_width, head_width)
        value_part = heads_slice(values_all, group_index, group_width, head_width)
        grad_part = heads_slice(grad_attn, group_index, group_width, head_width)
        scores = masked_scores(query_part, key_part, doc_mask)
        attn_prob = jnp.exp(scores - log_totals[group_index][..., None])
        grad_prob = jnp.einsum(
            "sqhd,skhd->shqk", grad_part, value_part, preferred_element_type=jnp.float32
        )
        row_dot = jnp.sum(attn_prob * grad_prob, axis=-1)
        grad_scores = (attn_prob * (grad_prob - row_dot[..., None]) * 0.125).astype(jnp.bfloat16)
        grad_query = jnp.einsum(
            "shqk,skhd->sqhd", grad_scores, key_part, preferred_element_type=jnp.float32
        )
        return (
            query_part,
            grad_part,
            attn_prob,
            grad_scores,
            grad_query.reshape(seq_count, tok_rows, group_width),
            row_dot,
        )

    def summed_group(group_index):
        query_part, grad_part, attn_prob, grad_scores, grad_query, row_dot = query_grads(
            group_index
        )
        grad_key = jnp.einsum(
            "shqk,sqhd->skhd", grad_scores, query_part, preferred_element_type=jnp.float32
        )
        grad_value = jnp.einsum(
            "shqk,sqhd->skhd",
            attn_prob.astype(jnp.bfloat16),
            grad_part,
            preferred_element_type=jnp.float32,
        )
        grad_key, grad_value = (
            lax.psum_scatter(
                grad_key.reshape(seq_count, seq_length, group_width).astype(jnp.bfloat16),
                "tok",
                scatter_dimension=1,
                tiled=True,
            ).astype(jnp.float32),
            lax.psum_scatter(
                grad_value.reshape(seq_count, seq_length, group_width).astype(jnp.bfloat16),
                "tok",
                scatter_dimension=1,
                tiled=True,
            ).astype(jnp.float32),
        )
        return (grad_query, grad_key, grad_value)

    query_parts, key_parts, value_parts = lax.map(summed_group, groups)
    grad_query = join_groups(query_parts)
    grad_key = join_groups(key_parts)
    grad_value = join_groups(value_parts)
    _, rotate_back = jax.vjp(lambda field: rotary(field, cosine, sine_part), query_pre)
    grad_query_pre = rotate_back(grad_query.reshape(head_shape))[0].reshape(
        seq_count, tok_rows, model_width
    )
    grad_key_pre = rotate_back(grad_key.reshape(head_shape))[0].reshape(
        seq_count, tok_rows, model_width
    )
    grad_qkv = jnp.concatenate([grad_query_pre, grad_key_pre, grad_value], axis=-1).astype(
        jnp.bfloat16
    )
    back_norm_one, down_qkv, up_qkv = project_back(
        grad_qkv, norm_one, narrow_qkv, w_qkv, picked[0], picked[1]
    )
    _, norm_one_back = jax.vjp(lambda field: layer_norm(field, gain_one), inputs)
    input_grad = (grad_mid + norm_one_back(back_norm_one)[0]).astype(jnp.bfloat16)
    terms = (down_qkv, up_qkv, down_out, up_out, down_in, up_in, down_o2, up_o2)
    summed = lax.psum(
        (
            spread_back(terms[0], onehot),
            spread_back(terms[1], onehot),
            spread_back(terms[2], onehot),
            spread_back(terms[3], onehot),
            spread_back(terms[4], onehot),
            spread_back(terms[5], onehot),
            spread_back(terms[6], onehot),
            spread_back(terms[7], onehot),
        ),
        ("seq", "tok"),
    )
    return (
        layer_out,
        input_grad,
        summed[0],
        summed[1],
        summed[2],
        summed[3],
        summed[4],
        summed[5],
        summed[6],
        summed[7],
    )


def solution(mesh):
    return jax.shard_map(
        body,
        mesh=mesh,
        in_specs=(
            P("seq", "tok", None),
            P("seq", "tok", None),
            P("seq", None),
            P("seq"),
            P("tok", "seq"),
            P("tok", "seq"),
            P("tok", "seq"),
            P("tok", "seq"),
            P("tok"),
            P("tok"),
            P(),
            P(),
            P(),
            P(),
            P(),
            P(),
            P(),
            P(),
        ),
        out_specs=(
            P("seq", "tok", None),
            P("seq", "tok", None),
            P(),
            P(),
            P(),
            P(),
            P(),
            P(),
            P(),
            P(),
        ),
        check_vma=False,
    )
```

profile of v0, /device:TPU:0, one launch (start us, length us, event | category | flops | bytes accessed | tf_op | source)
XLA Modules:
  0.0 1193.3 jit_solution(8519961414103918297)
XLA Ops:
  7.3 11.8 all_gather.45
  19.9 8.8 all_gather.54
  28.7 5.2 all-gather
  44.1 75.4 %all-gather.10.cloned.1.call-done = bf16[1024,3072]{1,0:T(8,128)(2,1)} async-done(((bf16[1024,384]{1,0:T(8,128)(2,1)}), bf16[1024,3072]{1,0:T(8,128)(2,1)}) %all-gather.10.cloned.1.call-update) | async-done | bytes 6291472 | tf_op jit(solution)/shard_map/all_gather | solution.py:150
  119.5 4.6 fusion.117
  142.6 4.2 add_convert_fusion.4
  149.3 6.4 all_gather.49
  156.6 5.5 all-gather.1
  169.6 59.1 %all-gather.22.cloned.1.call-done = bf16[2624,1024]{1,0:T(8,128)(2,1)} async-done(((bf16[2624,128]{1,0:T(8,128)(2,1)}), bf16[2624,1024]{1,0:T(8,128)(2,1)}) %all-gather.22.cloned.1.call-update) | async-done | bytes 5373968 | tf_op jit(solution)/shard_map/all_gather | solution.py:153
  228.7 4.2 fusion.71
  236.1 15.5 %all-gather.14.cloned.1.call-done = bf16[1,1024,1024]{2,1,0:T(8,128)(2,1)} async-done(((bf16[1,256,1024]{2,1,0:T(8,128)(2,1)}), bf16[1,1024,1024]{2,1,0:T(8,128)(2,1)}) %all-gather.14.cloned.1.call-update) | async-done | bytes 2097168 | tf_op jit(solution)/shard_map/all_gather | solution.py:174
  251.5 4.0 copy.83
  255.5 20.6 %all-gather.12.cloned.1.call-done = bf16[1,1024,1024]{2,1,0:T(8,128)(2,1)} async-done(((bf16[1,256,1024]{2,1,0:T(8,128)(2,1)}), bf16[1,1024,1024]{2,1,0:T(8,128)(2,1)}) %all-gather.12.cloned.1.call-update) | async-done | bytes 2097168 | tf_op jit(solution)/shard_map/all_gather | solution.py:175
  276.1 4.0 copy.81
  280.1 45.8 %while.30 = (s32[]{:T(128)}, bf16[8,1,256,128]{2,3,1,0:T(8,128)(2,1)S(1)}, f32[8,1,2,256]{3,2,1,0:T(2,128)}, s32[8]{0:T(128)S(1)}, bf16[1,1024,1024]{1,2,0:T(8,1...) while((s32[]{:T(128)}, ...), condition=%wide.region_5.6_spmd.clone.clone, body=%wide.region_2.5_spmd.clone.sunk.clone | while | flops 138149376 | bytes 8804011 | solution.py:192
  332.7 151.0 %all-gather.20.cloned.1.call-done = bf16[1024,5248]{0,1:T(8,128)(2,1)} async-done(((bf16[1024,656]{0,1:T(8,128)(2,1)}), bf16[1024,5248]{0,1:T(8,128)(2,1)}) %all-gather.20.cloned.1.call-update) | async-done | bytes 10747920 | tf_op jit(solution)/shard_map/all_gather | solution.py:152
  483.7 6.0 fusion.119
  491.5 6.7 fusion.48
  511.9 468.5 %while.31 = (s32[]{:T(128)}, f32[8,1,256,128]{2,3,1,0:T(8,128)}, f32[8,1,256,128]{2,3,1,0:T(8,128)}, bf16[8,1,256,128]{2,3,1,0:T(8,128)(2,1)}, s32[8]{0:T(128)S(...) while((s32[]{:T(128)}, f32[8,1,256,128]{2,3,1,0:T(8,128)}, ...), condition=%wide.region_14.15_spmd.clone.clone, body=%wide.region_10.14_spmd.clone.sunk.clone | while | flops 343477248 | bytes 23342488 | solution.py:284
  522.8 3.6 fusion.229
  529.1 3.6 fusion.228
  534.2 10.5 reduce-scatter.3.cloned.1.call-done
  546.3 21.2 %reduce-scatter.5.cloned.1.call-done = bf16[1,256,128]{1,2,0:T(8,128)(2,1)} async-done(((bf16[1,1024,128]{1,2,0:T(8,128)(2,1)}), bf16[1,256,128]{1,2,0:T(8,128)(2,1)}) %reduce-scatter.5.cloned.1.call-update) | async-done | bytes 65552 | tf_op jit(solution)/shard_map/while/body/eval_jaxpr/reduce_scatter | solution.py:275
  579.8 3.6 fusion.229
  586.1 3.5 fusion.228
  591.2 12.4 %reduce-scatter.3.cloned.1.call-done = bf16[1,256,128]{1,2,0:T(8,128)(2,1)} async-done(((bf16[1,1024,128]{1,2,0:T(8,128)(2,1)}), bf16[1,256,128]{1,2,0:T(8,128)(2,1)}) %reduce-scatter.3.cloned.1.call-update) | async-done | bytes 65552 | tf_op jit(solution)/shard_map/while/body/eval_jaxpr/reduce_scatter | solution.py:269
  605.1 21.1 %reduce-scatter.5.cloned.1.call-done = bf16[1,256,128]{1,2,0:T(8,128)(2,1)} async-done(((bf16[1,1024,128]{1,2,0:T(8,128)(2,1)}), bf16[1,256,128]{1,2,0:T(8,128)(2,1)}) %reduce-scatter.5.cloned.1.call-update) | async-done | bytes 65552 | tf_op jit(solution)/shard_map/while/body/eval_jaxpr/reduce_scatter | solution.py:275
  638.6 3.6 fusion.229
  650.0 12.4 %reduce-scatter.3.cloned.1.call-done = bf16[1,256,128]{1,2,0:T(8,128)(2,1)} async-done(((bf16[1,1024,128]{1,2,0:T(8,128)(2,1)}), bf16[1,256,128]{1,2,0:T(8,128)(2,1)}) %reduce-scatter.3.cloned.1.call-update) | async-done | bytes 65552 | tf_op jit(solution)/shard_map/while/body/eval_jaxpr/reduce_scatter | solution.py:269
  663.9 21.1 %reduce-scatter.5.cloned.1.call-done = bf16[1,256,128]{1,2,0:T(8,128)(2,1)} async-done(((bf16[1,1024,128]{1,2,0:T(8,128)(2,1)}), bf16[1,256,128]{1,2,0:T(8,128)(2,1)}) %reduce-scatter.5.cloned.1.call-update) | async-done | bytes 65552 | tf_op jit(solution)/shard_map/while/body/eval_jaxpr/reduce_scatter | solution.py:275
  697.4 3.6 fusion.229
  708.8 12.4 %reduce-scatter.3.cloned.1.call-done = bf16[1,256,128]{1,2,0:T(8,128)(2,1)} async-done(((bf16[1,1024,128]{1,2,0:T(8,128)(2,1)}), bf16[1,256,128]{1,2,0:T(8,128)(2,1)}) %reduce-scatter.3.cloned.1.call-update) | async-done | bytes 65552 | tf_op jit(solution)/shard_map/while/body/eval_jaxpr/reduce_scatter | solution.py:269
  722.7 21.0 %reduce-scatter.5.cloned.1.call-done = bf16[1,256,128]{1,2,0:T(8,128)(2,1)} async-done(((bf16[1,1024,128]{1,2,0:T(8,128)(2,1)}), bf16[1,256,128]{1,2,0:T(8,128)(2,1)}) %reduce-scatter.5.cloned.1.call-update) | async-done | bytes 65552 | tf_op jit(solution)/shard_map/while/body/eval_jaxpr/reduce_scatter | solution.py:275
  756.1 3.6 fusion.229
  767.4 12.4 %reduce-scatter.3.cloned.1.call-done = bf16[1,256,128]{1,2,0:T(8,128)(2,1)} async-done(((bf16[1,1024,128]{1,2,0:T(8,128)(2,1)}), bf16[1,256,128]{1,2,0:T(8,128)(2,1)}) %reduce-scatter.3.cloned.1.call-update) | async-done | bytes 65552 | tf_op jit(solution)/shard_map/while/body/eval_jaxpr/reduce_scatter | solution.py:269
  781.4 21.0 %reduce-scatter.5.cloned.1.call-done = bf16[1,256,128]{1,2,0:T(8,128)(2,1)} async-done(((bf16[1,1024,128]{1,2,0:T(8,128)(2,1)}), bf16[1,256,128]{1,2,0:T(8,128)(2,1)}) %reduce-scatter.5.cloned.1.call-update) | async-done | bytes 65552 | tf_op jit(solution)/shard_map/while/body/eval_jaxpr/reduce_scatter | solution.py:275
  814.8 3.6 fusion.229
  826.2 12.4 %reduce-scatter.3.cloned.1.call-done = bf16[1,256,128]{1,2,0:T(8,128)(2,1)} async-done(((bf16[1,1024,128]{1,2,0:T(8,128)(2,1)}), bf16[1,256,128]{1,2,0:T(8,128)(2,1)}) %reduce-scatter.3.cloned.1.call-update) | async-done | bytes 65552 | tf_op jit(solution)/shard_map/while/body/eval_jaxpr/reduce_scatter | solution.py:269
  840.1 21.2 %reduce-scatter.5.cloned.1.call-done = bf16[1,256,128]{1,2,0:T(8,128)(2,1)} async-done(((bf16[1,1024,128]{1,2,0:T(8,128)(2,1)}), bf16[1,256,128]{1,2,0:T(8,128)(2,1)}) %reduce-scatter.5.cloned.1.call-update) | async-done | bytes 65552 | tf_op jit(solution)/shard_map/while/body/eval_jaxpr/reduce_scatter | solution.py:275
  873.6 3.6 fusion.229
  884.9 12.4 %reduce-scatter.3.cloned.1.call-done = bf16[1,256,128]{1,2,0:T(8,128)(2,1)} async-done(((bf16[1,1024,128]{1,2,0:T(8,128)(2,1)}), bf16[1,256,128]{1,2,0:T(8,128)(2,1)}) %reduce-scatter.3.cloned.1.call-update) | async-done | bytes 65552 | tf_op jit(solution)/shard_map/while/body/eval_jaxpr/reduce_scatter | solution.py:269
  898.9 21.2 %reduce-scatter.5.cloned.1.call-done = bf16[1,256,128]{1,2,0:T(8,128)(2,1)} async-done(((bf16[1,1024,128]{1,2,0:T(8,128)(2,1)}), bf16[1,256,128]{1,2,0:T(8,128)(2,1)}) %reduce-scatter.5.cloned.1.call-update) | async-done | bytes 65552 | tf_op jit(solution)/shard_map/while/body/eval_jaxpr/reduce_scatter | solution.py:275
  932.4 3.6 fusion.229
  943.8 12.4 %reduce-scatter.3.cloned.1.call-done = bf16[1,256,128]{1,2,0:T(8,128)(2,1)} async-done(((bf16[1,1024,128]{1,2,0:T(8,128)(2,1)}), bf16[1,256,128]{1,2,0:T(8,128)(2,1)}) %reduce-scatter.3.cloned.1.call-update) | async-done | bytes 65552 | tf_op jit(solution)/shard_map/while/body/eval_jaxpr/reduce_scatter | solution.py:269
  957.7 21.2 %reduce-scatter.5.cloned.1.call-done = bf16[1,256,128]{1,2,0:T(8,128)(2,1)} async-done(((bf16[1,1024,128]{1,2,0:T(8,128)(2,1)}), bf16[1,256,128]{1,2,0:T(8,128)(2,1)}) %reduce-scatter.5.cloned.1.call-update) | async-done | bytes 65552 | tf_op jit(solution)/shard_map/while/body/eval_jaxpr/reduce_scatter | solution.py:275
  994.1 5.0 fusion.107
  1000.0 4.7 fusion.120
  1007.6 166.9 %all-reduce.7.cloned.1.call-done = (f32[8,16,1024]{2,1,0:T(8,128)}, f32[8,16,3072]{2,1,0:T(8,128)}, f32[8,16,1024]{2,1,0:T(8,128)}, f32[8,16,1024]{2,1,0:T(8,128...) async-done(((f32[8,16,1024]{2,1,0:T(8,128)}, f32[8,16,3072]{2,1,0:T(8,128)}, f32[8,16,1024]{2,1,0:T(8,128)}, ...) | async-done | bytes 8224784 | tf_op jit(solution)/shard_map/psum | solution.py:304
  (493 shorter events, 278.7 us)
Async XLA Ops:
  7.2 161.9 %copy-start = (bf16[8,16,5248]{2,1,0:T(8,128)(2,1)S(1)}, bf16[8,16,5248]{2,1,0:T(8,128)(2,1)}, u32[]{:S(2)}) copy-start(bf16[8,16,5248]{2,1,0:T(8,128)(2,1)} %param.37) | copy-start | bytes 4030468
  7.2 21.5 %copy-start.54 = (bf16[256]{0:T(256)(128)(2,1)S(1)}, bf16[256]{0:T(256)(128)(2,1)}, u32[]{:S(2)}) copy-start(bf16[256]{0:T(256)(128)(2,1)} %param.30) | copy-start | bytes 1540
  7.2 112.3 %all-gather.10.cloned.1.call-start = ((), (), s32[]{:S(2)}) async-start(), calls=%async_computation.2 | async-start | bytes 7077888 | tf_op jit(solution)/shard_map/all_gather | solution.py:150
  19.1 136.7 %all-gather.18.cloned.1.call-start = ((), (), s32[]{:S(2)}) async-start(), calls=%async_computation.6 | async-start | bytes 1679360 | tf_op jit(solution)/shard_map/all_gather | solution.py:144
  19.8 208.9 %all-gather.22.cloned.1.call-start = ((), (), s32[]{:S(2)}) async-start(), calls=%async_computation.8 | async-start | bytes 6045696 | tf_op jit(solution)/shard_map/all_gather | solution.py:153
  28.6 222.9 %all-gather.14.cloned.1.call-start = ((), (), s32[]{:S(2)}) async-start(), calls=%async_computation.4 | async-start | bytes 2621440 | tf_op jit(solution)/shard_map/all_gather | solution.py:174
  34.8 6.3 copy-start.29
  35.9 5.2 copy-start.3
  35.9 5.7 copy-start.49
  42.5 81.6 %copy-start.18 = (bf16[256,1024]{1,0:T(8,128)(2,1)}, bf16[256,1024]{1,0:T(8,128)(2,1)S(1)}, u32[]{:S(2)}) copy-start(bf16[256,1024]{1,0:T(8,128)(2,1)S(1)} %fusion.67) | copy-start | bytes 1572868
  142.6 6.7 copy-start.53
  146.9 9.7 copy-start.55
  146.9 15.2 %copy-start.40 = (s32[1,1024]{1,0:T(1,128)S(1)}, s32[1,1024]{1,0:T(1,128)}, u32[]{:S(2)}) copy-start(s32[1,1024]{1,0:T(1,128)} %param.24) | copy-start | bytes 12292
  146.9 15.2 %copy-start.50 = (bf16[8,16,1024]{2,1,0:T(8,128)(2,1)S(1)}, bf16[8,16,1024]{2,1,0:T(8,128)(2,1)}, u32[]{:S(2)}) copy-start(bf16[8,16,1024]{2,1,0:T(8,128)(2,1)} %param.34) | copy-start | bytes 786436
  146.9 129.2 %all-gather.12.cloned.1.call-start = ((), (), s32[]{:S(2)}) async-start(), calls=%async_computation.3 | async-start | bytes 2621440 | tf_op jit(solution)/shard_map/all_gather | solution.py:175
  149.2 18.1 %copy-start.13 = (bf16[1,256,1024]{2,1,0:T(8,128)(2,1)S(1)}, bf16[1,256,1024]{2,1,0:T(8,128)(2,1)}, u32[]{:S(2)}) copy-start(bf16[1,256,1024]{2,1,0:T(8,128)(2,1)} %param.23) | copy-start | bytes 1572868
  149.3 179.9 %all-gather.16.cloned.1.call-start = ((), (), s32[]{:S(2)}) async-start(), calls=%async_computation.5 | async-start | bytes 2359296 | tf_op jit(solution)/shard_map/all_gather | solution.py:151
  155.7 327.9 %all-gather.20.cloned.1.call-start = ((), (), s32[]{:S(2)}) async-start(), calls=%async_computation.7 | async-start | bytes 12091392 | tf_op jit(solution)/shard_map/all_gather | solution.py:152
  156.6 13.0 %copy-start.10 = (bf16[8,1,256,128]{2,3,1,0:T(8,128)(2,1)}, bf16[8,1,256,128]{2,3,1,0:T(8,128)(2,1)S(1)}, u32[]{:S(2)}) copy-start(bf16[8,1,256,128]{2,3,1,0:T(8,128)(2,1)S(1)} %fusion.114) | copy-start | bytes 1572868
  169.1 63.9 %copy-start.27 = (bf16[1,16,2624]{2,0,1:T(2,128)(2,1)}, bf16[1,16,2624]{2,0,1:T(2,128)(2,1)S(1)}, u32[]{:S(2)}) copy-start(bf16[1,16,2624]{2,0,1:T(2,128)(2,1)S(1)} %fusion.62) | copy-start | bytes 251908
  255.5 24.6 %copy-start.12 = (bf16[8,1,256,128]{2,3,1,0:T(8,128)(2,1)S(1)}, bf16[8,1,256,128]{2,3,1,0:T(8,128)(2,1)}, u32[]{:S(2)}) copy-start(bf16[8,1,256,128]{2,3,1,0:T(8,128)(2,1)} %copy-done.10) | copy-start | bytes 1572868
  280.1 45.8 %copy-start.48 = (bf16[1,16,1024]{2,0,1:T(2,128)(2,1)S(1)}, bf16[1,16,1024]{2,0,1:T(2,128)(2,1)}, u32[]{:S(2)}) copy-start(bf16[1,16,1024]{2,0,1:T(2,128)(2,1)} %fusion.79) | copy-start | bytes 98308
  511.9 32.9 %reduce-scatter.3.cloned.1.call-start = ((), (), s32[]{:S(2)}) async-start(), calls=%async_computation.10 | async-start | bytes 327680 | tf_op jit(solution)/shard_map/while/body/eval_jaxpr/reduce_scatter | solution.py:269
  522.8 6.3 copy-start.17
  526.4 41.0 %reduce-scatter.5.cloned.1.call-start = ((), (), s32[]{:S(2)}) async-start(), calls=%async_computation.11 | async-start | bytes 327680 | tf_op jit(solution)/shard_map/while/body/eval_jaxpr/reduce_scatter | solution.py:275
  568.9 34.7 %reduce-scatter.3.cloned.1.call-start = ((), (), s32[]{:S(2)}) async-start(), calls=%async_computation.10 | async-start | bytes 327680 | tf_op jit(solution)/shard_map/while/body/eval_jaxpr/reduce_scatter | solution.py:269
  579.8 6.3 copy-start.17
  583.4 42.8 %reduce-scatter.5.cloned.1.call-start = ((), (), s32[]{:S(2)}) async-start(), calls=%async_computation.11 | async-start | bytes 327680 | tf_op jit(solution)/shard_map/while/body/eval_jaxpr/reduce_scatter | solution.py:275
  627.7 34.7 %reduce-scatter.3.cloned.1.call-start = ((), (), s32[]{:S(2)}) async-start(), calls=%async_computation.10 | async-start | bytes 327680 | tf_op jit(solution)/shard_map/while/body/eval_jaxpr/reduce_scatter | solution.py:269
  638.6 6.3 copy-start.17
  642.2 42.8 %reduce-scatter.5.cloned.1.call-start = ((), (), s32[]{:S(2)}) async-start(), calls=%async_computation.11 | async-start | bytes 327680 | tf_op jit(solution)/shard_map/while/body/eval_jaxpr/reduce_scatter | solution.py:275
  686.5 34.7 %reduce-scatter.3.cloned.1.call-start = ((), (), s32[]{:S(2)}) async-start(), calls=%async_computation.10 | async-start | bytes 327680 | tf_op jit(solution)/shard_map/while/body/eval_jaxpr/reduce_scatter | solution.py:269
  697.4 6.3 copy-start.17
  701.0 42.7 %reduce-scatter.5.cloned.1.call-start = ((), (), s32[]{:S(2)}) async-start(), calls=%async_computation.11 | async-start | bytes 327680 | tf_op jit(solution)/shard_map/while/body/eval_jaxpr/reduce_scatter | solution.py:275
  745.2 34.7 %reduce-scatter.3.cloned.1.call-start = ((), (), s32[]{:S(2)}) async-start(), calls=%async_computation.10 | async-start | bytes 327680 | tf_op jit(solution)/shard_map/while/body/eval_jaxpr/reduce_scatter | solution.py:269
  756.0 6.3 copy-start.17
  759.6 42.8 %reduce-scatter.5.cloned.1.call-start = ((), (), s32[]{:S(2)}) async-start(), calls=%async_computation.11 | async-start | bytes 327680 | tf_op jit(solution)/shard_map/while/body/eval_jaxpr/reduce_scatter | solution.py:275
  803.9 34.7 %reduce-scatter.3.cloned.1.call-start = ((), (), s32[]{:S(2)}) async-start(), calls=%async_computation.10 | async-start | bytes 327680 | tf_op jit(solution)/shard_map/while/body/eval_jaxpr/reduce_scatter | solution.py:269
  814.8 6.3 copy-start.17
  818.4 42.9 %reduce-scatter.5.cloned.1.call-start = ((), (), s32[]{:S(2)}) async-start(), calls=%async_computation.11 | async-start | bytes 327680 | tf_op jit(solution)/shard_map/while/body/eval_jaxpr/reduce_scatter | solution.py:275
  862.7 34.6 %reduce-scatter.3.cloned.1.call-start = ((), (), s32[]{:S(2)}) async-start(), calls=%async_computation.10 | async-start | bytes 327680 | tf_op jit(solution)/shard_map/while/body/eval_jaxpr/reduce_scatter | solution.py:269
  873.6 6.3 copy-start.17
  877.2 42.9 %reduce-scatter.5.cloned.1.call-start = ((), (), s32[]{:S(2)}) async-start(), calls=%async_computation.11 | async-start | bytes 327680 | tf_op jit(solution)/shard_map/while/body/eval_jaxpr/reduce_scatter | solution.py:275
  921.5 34.7 %reduce-scatter.3.cloned.1.call-start = ((), (), s32[]{:S(2)}) async-start(), calls=%async_computation.10 | async-start | bytes 327680 | tf_op jit(solution)/shard_map/while/body/eval_jaxpr/reduce_scatter | solution.py:269
  932.4 6.3 copy-start.17
  936.0 42.9 %reduce-scatter.5.cloned.1.call-start = ((), (), s32[]{:S(2)}) async-start(), calls=%async_computation.11 | async-start | bytes 327680 | tf_op jit(solution)/shard_map/while/body/eval_jaxpr/reduce_scatter | solution.py:275
  980.4 194.1 %all-reduce.7.cloned.1.call-start = ((), (), s32[]{:S(2)}) async-start(), calls=%async_computation.9 | async-start | bytes 16515072 | tf_op jit(solution)/shard_map/psum | solution.py:304
  1174.5 5.6 copy-start.34
  (56 other events, 126.2 us)
Sparse Core Ops, SparseCore 0:
  19.2 100.2 all-gather.9
  121.1 16.6 all-gather.17
  139.8 88.8 all-gather.21
  230.7 20.7 all-gather.13
  253.5 22.5 all-gather.11
  278.0 51.1 all-gather.15
  331.4 152.2 all-gather.19
  526.5 18.2 reduce-scatter.2
  547.4 19.9 reduce-scatter.4
  583.5 20.0 reduce-scatter.2
  606.2 19.9 reduce-scatter.4
  642.3 20.0 reduce-scatter.2
  665.0 19.9 reduce-scatter.4
  701.1 20.0 reduce-scatter.2
  723.7 20.0 reduce-scatter.4
  759.8 20.0 reduce-scatter.2
  782.3 20.0 reduce-scatter.4
  818.5 20.0 reduce-scatter.2
  841.2 20.0 reduce-scatter.4
  877.3 20.0 reduce-scatter.2
  900.0 20.0 reduce-scatter.4
  936.1 20.0 reduce-scatter.2
  958.8 20.0 reduce-scatter.4
  994.2 180.2 all-reduce.6
where the time goes:
time: 1200 us; the launch traced here: 1190 us
  waiting for transfers between devices  760 us (63%)
  matrix products  161 us (13%)
  local copies, waits for them, and re-layouts  125 us (10%)
  other arithmetic  65.6 us (5%)
  blocking collectives  37.7 us (3%)
  loops' own time  27.1 us (2%)
  between operations  15.8 us (1%)
    reduce_scatter x8, waiting for transfers between devices, summed_group(): lax.psum_scatter(grad_value.reshape(seq_count, seq_length, group_width).a...  169 us
    psum x1, waiting for transfers between devices, body(): lax.psum((spread_back(terms[0], onehot), spread_back(terms[1], onehot), s...  167 us
    all_gather x1, waiting for transfers between devices, body(): lax.all_gather(tok_parts[2], 'seq', axis=1, tiled=True)  151 us
    reduce_scatter x8, waiting for transfers between devices, summed_group(): lax.psum_scatter(grad_key.reshape(seq_count, seq_length, group_width).ast...  97.5 us
    all_gather x1, waiting for transfers between devices, body(): lax.all_gather(tok_parts[0], 'seq', axis=1, tiled=True)  75.4 us
    all_gather x1, waiting for transfers between devices, body(): lax.all_gather(tok_parts[3], 'seq', axis=1, tiled=True)  59.1 us
    dynamic_slice x48, local copies, waits for them, and re-layouts, heads_slice(): lax.dynamic_slice_in_dim(source, group_index * group_width, group_width, 2)  48.9 us
    dot_general x8, matrix products, summed_group(): jnp.einsum('shqk,sqhd->skhd', grad_scores, query_part, preferred_element_...  28.5 us
  transfers between devices with their start and end apart: 24, of which 23 were waited for; matrix products, arithmetic and copies ran while one was open for 16% of the time, Pallas kernels for 0%

commit v1 on v0

--- a/solution.py
+++ b/solution.py
@@ -10,6 +10,22 @@
 EPS = 1e-05
 THETA = 160000.0
 HIGH = lax.Precision.HIGHEST
+
+
+def collect(x, axis, dim):
+    ways, here, lap = (lax.axis_size(axis), lax.axis_index(axis), x.shape[dim])
+    lengths = [n * ways if d == dim else n for d, n in enumerate(x.shape)]
+    full = lax.dynamic_update_slice_in_dim(jnp.zeros(lengths, x.dtype), x, here * lap, axis=dim)
+    going_up = going_down = x
+    for far in range(1, ways // 2 + 1):
+        going_up = lax.ppermute(going_up, axis, [(d, (d + 1) % ways) for d in range(ways)])
+        full = lax.dynamic_update_slice_in_dim(full, going_up, (here - far) % ways * lap, axis=dim)
+        if 2 * far < ways:
+            going_down = lax.ppermute(going_down, axis, [(d, (d - 1) % ways) for d in range(ways)])
+            full = lax.dynamic_update_slice_in_dim(
+                full, going_down, (here + far) % ways * lap, axis=dim
+            )
+    return full
 
 
 def layer_norm(values, gain_vec):
@@ -149,7 +165,7 @@
     w_qkv, w_out, w_in, w_out2 = (
         lax.all_gather(tok_parts[0], "seq", axis=1, tiled=True),
         lax.all_gather(tok_parts[1], "seq", axis=1, tiled=True),
-        lax.all_gather(tok_parts[2], "seq", axis=1, tiled=True),
+        collect(tok_parts[2], "seq", 1),
         lax.all_gather(tok_parts[3], "seq", axis=1, tiled=True),
     )
     gain_one = tok_parts[4].astype(jnp.float32)

time: 1200 us -> 1290 us (1.075)
  waiting for transfers between devices: 760 us -> 796 us
  local copies, waits for them, and re-layouts: 125 us -> 149 us
  starting transfers between devices: 0.87 us -> 16.6 us
    ppermute x0 -> x7, waiting for transfers between devices: none -> 183 us  [the longest x4 180 us: collect(): lax.ppermute(going_up, axis, [(d, (d + 1) % ways) for d in range(ways)])]
    all_gather x1, waiting for transfers between devices: 59.1 us -> 0.01 us  [body(): lax.all_gather(tok_parts[3], 'seq', axis=1, tiled=True)]
    all_gather x1, waiting for transfers between devices: 151 us -> 99 us  [body(): lax.all_gather(back_parts[2], 'seq', axis=1, tiled=True)]
    all_gather x1, waiting for transfers between devices: 20.6 us -> 0.01 us  [body(): lax.all_gather(value_low, 'tok', axis=1, tiled=True)]
    dynamic_update_slice x0 -> x8, local copies, waits for them, and re-layouts: none -> 18.8 us  [the longest x4 10.1 us: collect(): lax.dynamic_update_slice_in_dim(full, going_up, (here - far) % ways * lap...]
    ppermute x0 -> x7, starting transfers between devices: none -> 16 us  [the longest x4 8.97 us: collect(): lax.ppermute(going_up, axis, [(d, (d + 1) % ways) for d in range(ways)])]
    all_gather x1, waiting for transfers between devices: 15.5 us -> 0.01 us  [body(): lax.all_gather(key_low, 'tok', axis=1, tiled=True)]
    unnamed x125 -> x127, local copies, waits for them, and re-layouts: 28.1 us -> 25.8 us
  transfers between devices with their start and end apart: 24 -> 31, of which waited for: 23 -> 23; matrix products, arithmetic and copies ran while one was open for 16% -> 18% of each run, Pallas kernels for 0% -> 0%
where the time goes in v1:
time: 1290 us; the launch traced here: 1280 us
  waiting for transfers between devices  796 us (62%)
  matrix products  165 us (13%)
  local copies, waits for them, and re-layouts  149 us (12%)
  other arithmetic  64.4 us (5%)
  blocking collectives  47.9 us (4%)
  loops' own time  27.1 us (2%)
  starting transfers between devices  16.6 us (1%)
  between operations  15.9 us (1%)
    ppermute x4, waiting for transfers between devices, collect(): lax.ppermute(going_up, axis, [(d, (d + 1) % ways) for d in range(ways)])  180 us
    reduce_scatter x8, waiting for transfers between devices, summed_group(): lax.psum_scatter(grad_value.reshape(seq_count, seq_length, group_width).a...  174 us
    psum x1, waiting for transfers between devices, body(): lax.psum((spread_back(terms[0], onehot), spread_back(terms[1], onehot), s...  166 us
    all_gather x1, waiting for transfers between devices, body(): lax.all_gather(back_parts[2], 'seq', axis=1, tiled=True)  99 us
    reduce_scatter x8, waiting for transfers between devices, summed_group(): lax.psum_scatter(grad_key.reshape(seq_count, seq_length, group_width).ast...  97.3 us
    all_gather x1, waiting for transfers between devices, body(): lax.all_gather(tok_parts[0], 'seq', axis=1, tiled=True)  75.4 us
    dynamic_slice x48, local copies, waits for them, and re-layouts, heads_slice(): lax.dynamic_slice_in_dim(source, group_index * group_width, group_width, 2)  49.1 us
    dot_general x8, matrix products, summed_group(): jnp.einsum('shqk,sqhd->skhd', grad_scores, query_part, preferred_element_...  28.5 us
  transfers between devices with their start and end apart: 31, of which 23 were waited for; matrix products, arithmetic and copies ran while one was open for 18% of the time, Pallas kernels for 0%

profile of v1, /device:TPU:0, one launch (start us, length us, event | category | flops | bytes accessed | tf_op | source)
XLA Modules:
  0.0 1281.5 jit_solution(13585343045302111767)
XLA Ops:
  7.3 11.8 all_gather.44
  19.9 8.8 all_gather.52
  28.7 5.2 all-gather
  44.1 75.4 %all-gather.10.cloned.1.call-done = bf16[1024,3072]{1,0:T(8,128)(2,1)} async-done(((bf16[1024,384]{1,0:T(8,128)(2,1)}), bf16[1024,3072]{1,0:T(8,128)(2,1)}) %all-gather.10.cloned.1.call-update) | async-done | bytes 6291472 | tf_op jit(solution)/shard_map/all_gather | solution.py:166
  119.5 4.6 fusion.118
  144.4 4.3 add_convert_fusion.4
  152.6 6.2 all_gather.48
  162.2 53.6 %collective-permute-done = bf16[1024,656]{0,1:T(8,128)(2,1)} collective-permute-done((bf16[1024,656]{0,1:T(8,128)(2,1)}, bf16[1024,656]{0,1:T(8,128)(2,1)}, u32[]{:S(2)}, u32[]{:S(2)}) %collective-permute-start) | collective-permute-done | bytes 1343520 | tf_op jit(solution)/shard_map/ppermute | solution.py:21
  222.3 77.5 %collective-permute-done.2 = bf16[1024,656]{0,1:T(8,128)(2,1)} collective-permute-done((bf16[1024,656]{0,1:T(8,128)(2,1)}, bf16[1024,656]{0,1:T(8,128)(2,1)}, u32[]{:S(2)}, u32[]{:S(2)}) %collective-permute-start.2) | collective-permute-done | bytes 1343520 | tf_op jit(solution)/shard_map/ppermute | solution.py:21
  310.5 49.4 %collective-permute-done.4 = bf16[1024,656]{0,1:T(8,128)(2,1)} collective-permute-done((bf16[1024,656]{0,1:T(8,128)(2,1)}, bf16[1024,656]{0,1:T(8,128)(2,1)}, u32[]{:S(2)}, u32[]{:S(2)}) %collective-permute-start.4) | collective-permute-done | bytes 1343520 | tf_op jit(solution)/shard_map/ppermute | solution.py:21
  362.4 16.0 %all-gather.1 = bf16[4,1,256]{2,1,0:T(2,128)(2,1)S(1)} all-gather(bf16[1,1,256]{2,1,0:T(2,128)(2,1)S(1)} %reshape.799), channel_id=1, replica_groups=mesh['seq'=8,'tok'=4] {'tok'}, dimensions={0}, use_global_device_ids=true | all-gather | bytes 2560 | tf_op jit(solution)/shard_map/all_gather | solution.py:163
  378.9 5.3 broadcast_in_dim.97
  403.0 4.2 fusion.71
  410.4 4.0 copy.83
  414.3 4.0 copy.81
  418.4 45.8 %while.30 = (s32[]{:T(128)}, bf16[8,1,256,128]{2,3,1,0:T(8,128)(2,1)S(1)}, f32[8,1,2,256]{3,2,1,0:T(2,128)}, s32[8]{0:T(128)S(1)}, bf16[1,1024,1024]{1,2,0:T(8,1...) while((s32[]{:T(128)}, ...), condition=%wide.region_5.6_spmd.clone.clone, body=%wide.region_2.5_spmd.clone.sunk.clone | while | flops 138149376 | bytes 8804011 | solution.py:208
  468.9 6.0 fusion.26
  474.8 6.5 fusion.48
  488.9 99.0 %all-gather.22.cloned.1.call-done = bf16[1024,5248]{0,1:T(8,128)(2,1)} async-done(((bf16[1024,656]{0,1:T(8,128)(2,1)}), bf16[1024,5248]{0,1:T(8,128)(2,1)}) %all-gather.22.cloned.1.call-update) | async-done | bytes 10747920 | tf_op jit(solution)/shard_map/all_gather | solution.py:226
  587.9 6.7 fusion.61
  600.6 473.0 %while.31 = (s32[]{:T(128)}, f32[8,1,256,128]{2,3,1,0:T(8,128)}, f32[8,1,256,128]{2,3,1,0:T(8,128)}, bf16[8,1,256,128]{2,3,1,0:T(8,128)(2,1)}, s32[8]{0:T(128)S(...) while((s32[]{:T(128)}, f32[8,1,256,128]{2,3,1,0:T(8,128)}, ...), condition=%wide.region_14.15_spmd.clone.clone, body=%wide.region_10.14_spmd.clone.sunk.clone | while | flops 343477248 | bytes 23342488 | solution.py:300
  611.4 3.6 fusion.229
  617.7 3.6 fusion.228
  622.8 10.5 reduce-scatter.3.cloned.1.call-done
  634.9 21.8 %reduce-scatter.5.cloned.1.call-done = bf16[1,256,128]{1,2,0:T(8,128)(2,1)} async-done(((bf16[1,1024,128]{1,2,0:T(8,128)(2,1)}), bf16[1,256,128]{1,2,0:T(8,128)(2,1)}) %reduce-scatter.5.cloned.1.call-update) | async-done | bytes 65552 | tf_op jit(solution)/shard_map/while/body/eval_jaxpr/reduce_scatter | solution.py:291
  669.0 3.6 fusion.229
  680.4 12.4 reduce-scatter.3.cloned.1.call-done
  694.3 21.8 %reduce-scatter.5.cloned.1.call-done = bf16[1,256,128]{1,2,0:T(8,128)(2,1)} async-done(((bf16[1,1024,128]{1,2,0:T(8,128)(2,1)}), bf16[1,256,128]{1,2,0:T(8,128)(2,1)}) %reduce-scatter.5.cloned.1.call-update) | async-done | bytes 65552 | tf_op jit(solution)/shard_map/while/body/eval_jaxpr/reduce_scatter | solution.py:291
  728.4 3.6 fusion.229
  739.8 12.4 reduce-scatter.3.cloned.1.call-done
  753.6 21.7 %reduce-scatter.5.cloned.1.call-done = bf16[1,256,128]{1,2,0:T(8,128)(2,1)} async-done(((bf16[1,1024,128]{1,2,0:T(8,128)(2,1)}), bf16[1,256,128]{1,2,0:T(8,128)(2,1)}) %reduce-scatter.5.cloned.1.call-update) | async-done | bytes 65552 | tf_op jit(solution)/shard_map/while/body/eval_jaxpr/reduce_scatter | solution.py:291
  787.8 3.6 fusion.229
  799.2 12.4 reduce-scatter.3.cloned.1.call-done
  813.0 21.6 %reduce-scatter.5.cloned.1.call-done = bf16[1,256,128]{1,2,0:T(8,128)(2,1)} async-done(((bf16[1,1024,128]{1,2,0:T(8,128)(2,1)}), bf16[1,256,128]{1,2,0:T(8,128)(2,1)}) %reduce-scatter.5.cloned.1.call-update) | async-done | bytes 65552 | tf_op jit(solution)/shard_map/while/body/eval_jaxpr/reduce_scatter | solution.py:291
  858.4 12.4 reduce-scatter.3.cloned.1.call-done
  872.3 21.6 %reduce-scatter.5.cloned.1.call-done = bf16[1,256,128]{1,2,0:T(8,128)(2,1)} async-done(((bf16[1,1024,128]{1,2,0:T(8,128)(2,1)}), bf16[1,256,128]{1,2,0:T(8,128)(2,1)}) %reduce-scatter.5.cloned.1.call-update) | async-done | bytes 65552 | tf_op jit(solution)/shard_map/while/body/eval_jaxpr/reduce_scatter | solution.py:291
  906.3 3.6 fusion.229
  917.6 12.4 reduce-scatter.3.cloned.1.call-done
  931.5 21.7 %reduce-scatter.5.cloned.1.call-done = bf16[1,256,128]{1,2,0:T(8,128)(2,1)} async-done(((bf16[1,1024,128]{1,2,0:T(8,128)(2,1)}), bf16[1,256,128]{1,2,0:T(8,128)(2,1)}) %reduce-scatter.5.cloned.1.call-update) | async-done | bytes 65552 | tf_op jit(solution)/shard_map/while/body/eval_jaxpr/reduce_scatter | solution.py:291
  965.7 3.6 fusion.229
  977.0 12.4 reduce-scatter.3.cloned.1.call-done
  990.9 21.8 %reduce-scatter.5.cloned.1.call-done = bf16[1,256,128]{1,2,0:T(8,128)(2,1)} async-done(((bf16[1,1024,128]{1,2,0:T(8,128)(2,1)}), bf16[1,256,128]{1,2,0:T(8,128)(2,1)}) %reduce-scatter.5.cloned.1.call-update) | async-done | bytes 65552 | tf_op jit(solution)/shard_map/while/body/eval_jaxpr/reduce_scatter | solution.py:291
  1025.1 3.6 fusion.229
  1036.4 12.4 reduce-scatter.3.cloned.1.call-done
  1050.4 21.7 %reduce-scatter.5.cloned.1.call-done = bf16[1,256,128]{1,2,0:T(8,128)(2,1)} async-done(((bf16[1,1024,128]{1,2,0:T(8,128)(2,1)}), bf16[1,256,128]{1,2,0:T(8,128)(2,1)}) %reduce-scatter.5.cloned.1.call-update) | async-done | bytes 65552 | tf_op jit(solution)/shard_map/while/body/eval_jaxpr/reduce_scatter | solution.py:291
  1083.4 4.3 fusion.120
  1088.9 4.8 fusion.108
  1096.4 166.1 %all-reduce.7.cloned.1.call-done = (f32[8,16,1024]{2,1,0:T(8,128)}, f32[8,16,3072]{2,1,0:T(8,128)}, f32[8,16,1024]{2,1,0:T(8,128)}, f32[8,16,1024]{2,1,0:T(8,128...) async-done(((f32[8,16,1024]{2,1,0:T(8,128)}, f32[8,16,3072]{2,1,0:T(8,128)}, f32[8,16,1024]{2,1,0:T(8,128)}, ...) | async-done | bytes 8224784 | tf_op jit(solution)/shard_map/psum | solution.py:320
  (517 shorter events, 315.1 us)
Async XLA Ops:
  7.2 371.2 %copy-start = (bf16[8,16,5248]{2,1,0:T(8,128)(2,1)S(1)}, bf16[8,16,5248]{2,1,0:T(8,128)(2,1)}, u32[]{:S(2)}) copy-start(bf16[8,16,5248]{2,1,0:T(8,128)(2,1)} %param.37) | copy-start | bytes 4030468
  7.2 21.5 %copy-start.58 = (bf16[256]{0:T(256)(128)(2,1)S(1)}, bf16[256]{0:T(256)(128)(2,1)}, u32[]{:S(2)}) copy-start(bf16[256]{0:T(256)(128)(2,1)} %param.30) | copy-start | bytes 1540
  7.2 112.3 %all-gather.10.cloned.1.call-start = ((), (), s32[]{:S(2)}) async-start(), calls=%async_computation.2 | async-start | bytes 7077888 | tf_op jit(solution)/shard_map/all_gather | solution.py:166
  19.1 132.0 %all-gather.18.cloned.1.call-start = ((), (), s32[]{:S(2)}) async-start(), calls=%async_computation.6 | async-start | bytes 1679360 | tf_op jit(solution)/shard_map/all_gather | solution.py:160
  19.8 383.2 %all-gather.20.cloned.1.call-start = ((), (), s32[]{:S(2)}) async-start(), calls=%async_computation.7 | async-start | bytes 6045696 | tf_op jit(solution)/shard_map/all_gather | solution.py:169
  28.6 381.7 %all-gather.14.cloned.1.call-start = ((), (), s32[]{:S(2)}) async-start(), calls=%async_computation.4 | async-start | bytes 2621440 | tf_op jit(solution)/shard_map/all_gather | solution.py:190
  34.8 6.3 copy-start.29
  42.5 81.6 %copy-start.18 = (bf16[256,1024]{1,0:T(8,128)(2,1)}, bf16[256,1024]{1,0:T(8,128)(2,1)S(1)}, u32[]{:S(2)}) copy-start(bf16[256,1024]{1,0:T(8,128)(2,1)S(1)} %fusion.67) | copy-start | bytes 1572868
  144.4 8.2 copy-start.57
  148.7 72.7 %copy-start.53 = (bf16[8,16,1024]{2,1,0:T(8,128)(2,1)S(1)}, bf16[8,16,1024]{2,1,0:T(8,128)(2,1)}, u32[]{:S(2)}) copy-start(bf16[8,16,1024]{2,1,0:T(8,128)(2,1)} %param.34) | copy-start | bytes 786436
  148.7 153.7 %copy-start.54 = (bf16[8,16,1024]{2,1,0:T(8,128)(2,1)S(1)}, bf16[8,16,1024]{2,1,0:T(8,128)(2,1)}, u32[]{:S(2)}) copy-start(bf16[8,16,1024]{2,1,0:T(8,128)(2,1)} %param.35) | copy-start | bytes 786436
  148.7 157.0 %copy-start.13 = (bf16[1,256,1024]{2,1,0:T(8,128)(2,1)S(1)}, bf16[1,256,1024]{2,1,0:T(8,128)(2,1)}, u32[]{:S(2)}) copy-start(bf16[1,256,1024]{2,1,0:T(8,128)(2,1)} %param.23) | copy-start | bytes 1572868
  148.7 161.8 %copy-start.42 = (s32[1,1024]{1,0:T(1,128)S(1)}, s32[1,1024]{1,0:T(1,128)}, u32[]{:S(2)}) copy-start(s32[1,1024]{1,0:T(1,128)} %param.24) | copy-start | bytes 12292
  148.7 265.6 %all-gather.12.cloned.1.call-start = ((), (), s32[]{:S(2)}) async-start(), calls=%async_computation.3 | async-start | bytes 2621440 | tf_op jit(solution)/shard_map/all_gather | solution.py:191
  151.0 211.3 %copy-start.59 = (bf16[256]{0:T(256)(128)(2,1)S(1)}, bf16[256]{0:T(256)(128)(2,1)}, u32[]{:S(2)}) copy-start(bf16[256]{0:T(256)(128)(2,1)} %param.31) | copy-start | bytes 1540
  151.0 313.4 %all-gather.16.cloned.1.call-start = ((), (), s32[]{:S(2)}) async-start(), calls=%async_computation.5 | async-start | bytes 2359296 | tf_op jit(solution)/shard_map/all_gather | solution.py:167
  151.1 64.7 %collective-permute-start = (bf16[1024,656]{0,1:T(8,128)(2,1)}, bf16[1024,656]{0,1:T(8,128)(2,1)}, u32[]{:S(2)}, u32[]{:S(2)}) collective-permute-start(bf16[1024,656]{0,1:T(8,128)(2,1)} %all-gather.18.cloned.1.call-done), channel_id=1, source_target_pairs={{0,4},{4,8},{8,12},{12,16},{16,20},{20,24},{24,28},{28,0},{1,5},{5... | collective-permute-start | bytes 4030472 | tf_op jit(solution)/shard_map/ppermute | solution.py:21
  158.9 429.0 %all-gather.22.cloned.1.call-start = ((), (), s32[]{:S(2)}) async-start(), calls=%async_computation.8 | async-start | bytes 12091392 | tf_op jit(solution)/shard_map/all_gather | solution.py:226
  158.9 61.9 %collective-permute-start.1 = (bf16[1024,656]{0,1:T(8,128)(2,1)}, bf16[1024,656]{0,1:T(8,128)(2,1)}, u32[]{:S(2)}, u32[]{:S(2)}) collective-permute-start(bf16[1024,656]{0,1:T(8,128)(2,1)} %all-gather.18.cloned.1.call-done), channel_id=1, source_target_pairs={{0,28},{4,0},{8,4},{12,8},{16,12},{20,16},{24,20},{28,24},{1,29},{... | collective-permute-start | bytes 4030472 | tf_op jit(solution)/shard_map/ppermute | solution.py:24
  215.8 84.0 %collective-permute-start.2 = (bf16[1024,656]{0,1:T(8,128)(2,1)}, bf16[1024,656]{0,1:T(8,128)(2,1)}, u32[]{:S(2)}, u32[]{:S(2)}) collective-permute-start(bf16[1024,656]{0,1:T(8,128)(2,1)} %collective-permute-done), channel_id=1, source_target_pairs={{0,4},{4,8},{8,12},{12,16},{16,20},{20,24},{24,28},{28,0},{1,5},{5... | collective-permute-start | bytes 4030472 | tf_op jit(solution)/shard_map/ppermute | solution.py:21
  220.8 86.6 %collective-permute-start.3 = (bf16[1024,656]{0,1:T(8,128)(2,1)}, bf16[1024,656]{0,1:T(8,128)(2,1)}, u32[]{:S(2)}, u32[]{:S(2)}) collective-permute-start(bf16[1024,656]{0,1:T(8,128)(2,1)} %collective-permute-done.1), channel_id=1, source_target_pairs={{0,28},{4,0},{8,4},{12,8},{16,12},{20,16},{24,20},{28,24},{1,29},{... | collective-permute-start | bytes 4030472 | tf_op jit(solution)/shard_map/ppermute | solution.py:24
  299.8 60.0 %collective-permute-start.4 = (bf16[1024,656]{0,1:T(8,128)(2,1)}, bf16[1024,656]{0,1:T(8,128)(2,1)}, u32[]{:S(2)}, u32[]{:S(2)}) collective-permute-start(bf16[1024,656]{0,1:T(8,128)(2,1)} %collective-permute-done.2), channel_id=1, source_target_pairs={{0,4},{4,8},{8,12},{12,16},{16,20},{20,24},{24,28},{28,0},{1,5},{5... | collective-permute-start | bytes 4030472 | tf_op jit(solution)/shard_map/ppermute | solution.py:21
  302.4 76.5 %copy-start.10 = (bf16[8,1,256,128]{2,3,1,0:T(8,128)(2,1)}, bf16[8,1,256,128]{2,3,1,0:T(8,128)(2,1)S(1)}, u32[]{:S(2)}) copy-start(bf16[8,1,256,128]{2,3,1,0:T(8,128)(2,1)S(1)} %fusion.115) | copy-start | bytes 1572868
  305.7 72.6 %copy-start.55 = (bf16[1,16,1024]{2,0,1:T(2,128)(2,1)}, bf16[1,16,1024]{2,0,1:T(2,128)(2,1)S(1)}, u32[]{:S(2)}) copy-start(bf16[1,16,1024]{2,0,1:T(2,128)(2,1)S(1)} %fusion.73) | copy-start | bytes 98308
  307.4 90.6 %collective-permute-start.5 = (bf16[1024,656]{0,1:T(8,128)(2,1)}, bf16[1024,656]{0,1:T(8,128)(2,1)}, u32[]{:S(2)}, u32[]{:S(2)}) collective-permute-start(bf16[1024,656]{0,1:T(8,128)(2,1)} %collective-permute-done.3), channel_id=1, source_target_pairs={{0,28},{4,0},{8,4},{12,8},{16,12},{20,16},{24,20},{28,24},{1,29},{... | collective-permute-start | bytes 4030472 | tf_op jit(solution)/shard_map/ppermute | solution.py:24
  359.9 40.6 %collective-permute-start.6 = (bf16[1024,656]{0,1:T(8,128)(2,1)}, bf16[1024,656]{0,1:T(8,128)(2,1)}, u32[]{:S(2)}, u32[]{:S(2)}) collective-permute-start(bf16[1024,656]{0,1:T(8,128)(2,1)} %collective-permute-done.4), channel_id=1, source_target_pairs={{0,4},{4,8},{8,12},{12,16},{16,20},{20,24},{24,28},{28,0},{1,5},{5... | collective-permute-start | bytes 4030472 | tf_op jit(solution)/shard_map/ppermute | solution.py:21
  418.4 45.9 %copy-start.46 = (bf16[1,16,1024]{2,0,1:T(2,128)(2,1)S(1)}, bf16[1,16,1024]{2,0,1:T(2,128)(2,1)}, u32[]{:S(2)}) copy-start(bf16[1,16,1024]{2,0,1:T(2,128)(2,1)} %fusion.79) | copy-start | bytes 98308
  600.6 32.8 %reduce-scatter.3.cloned.1.call-start = ((), (), s32[]{:S(2)}) async-start(), calls=%async_computation.10 | async-start | bytes 327680 | tf_op jit(solution)/shard_map/while/body/eval_jaxpr/reduce_scatter | solution.py:285
  615.0 41.6 %reduce-scatter.5.cloned.1.call-start = ((), (), s32[]{:S(2)}) async-start(), calls=%async_computation.11 | async-start | bytes 327680 | tf_op jit(solution)/shard_map/while/body/eval_jaxpr/reduce_scatter | solution.py:291
  658.1 34.7 %reduce-scatter.3.cloned.1.call-start = ((), (), s32[]{:S(2)}) async-start(), calls=%async_computation.10 | async-start | bytes 327680 | tf_op jit(solution)/shard_map/while/body/eval_jaxpr/reduce_scatter | solution.py:285
  669.0 6.3 copy-start.16
  672.6 43.4 %reduce-scatter.5.cloned.1.call-start = ((), (), s32[]{:S(2)}) async-start(), calls=%async_computation.11 | async-start | bytes 327680 | tf_op jit(solution)/shard_map/while/body/eval_jaxpr/reduce_scatter | solution.py:291
  717.5 34.6 %reduce-scatter.3.cloned.1.call-start = ((), (), s32[]{:S(2)}) async-start(), calls=%async_computation.10 | async-start | bytes 327680 | tf_op jit(solution)/shard_map/while/body/eval_jaxpr/reduce_scatter | solution.py:285
  732.0 43.4 %reduce-scatter.5.cloned.1.call-start = ((), (), s32[]{:S(2)}) async-start(), calls=%async_computation.11 | async-start | bytes 327680 | tf_op jit(solution)/shard_map/while/body/eval_jaxpr/reduce_scatter | solution.py:291
  776.9 34.7 %reduce-scatter.3.cloned.1.call-start = ((), (), s32[]{:S(2)}) async-start(), calls=%async_computation.10 | async-start | bytes 327680 | tf_op jit(solution)/shard_map/while/body/eval_jaxpr/reduce_scatter | solution.py:285
  787.8 6.3 copy-start.16
  791.4 43.3 %reduce-scatter.5.cloned.1.call-start = ((), (), s32[]{:S(2)}) async-start(), calls=%async_computation.11 | async-start | bytes 327680 | tf_op jit(solution)/shard_map/while/body/eval_jaxpr/reduce_scatter | solution.py:291
  836.1 34.7 %reduce-scatter.3.cloned.1.call-start = ((), (), s32[]{:S(2)}) async-start(), calls=%async_computation.10 | async-start | bytes 327680 | tf_op jit(solution)/shard_map/while/body/eval_jaxpr/reduce_scatter | solution.py:285
  850.7 43.3 %reduce-scatter.5.cloned.1.call-start = ((), (), s32[]{:S(2)}) async-start(), calls=%async_computation.11 | async-start | bytes 327680 | tf_op jit(solution)/shard_map/while/body/eval_jaxpr/reduce_scatter | solution.py:291
  895.4 34.6 %reduce-scatter.3.cloned.1.call-start = ((), (), s32[]{:S(2)}) async-start(), calls=%async_computation.10 | async-start | bytes 327680 | tf_op jit(solution)/shard_map/while/body/eval_jaxpr/reduce_scatter | solution.py:285
  909.9 43.4 %reduce-scatter.5.cloned.1.call-start = ((), (), s32[]{:S(2)}) async-start(), calls=%async_computation.11 | async-start | bytes 327680 | tf_op jit(solution)/shard_map/while/body/eval_jaxpr/reduce_scatter | solution.py:291
  954.7 34.7 %reduce-scatter.3.cloned.1.call-start = ((), (), s32[]{:S(2)}) async-start(), calls=%async_computation.10 | async-start | bytes 327680 | tf_op jit(solution)/shard_map/while/body/eval_jaxpr/reduce_scatter | solution.py:285
  965.7 6.3 copy-start.16
  969.3 43.4 %reduce-scatter.5.cloned.1.call-start = ((), (), s32[]{:S(2)}) async-start(), calls=%async_computation.11 | async-start | bytes 327680 | tf_op jit(solution)/shard_map/while/body/eval_jaxpr/reduce_scatter | solution.py:291
  1014.2 34.7 %reduce-scatter.3.cloned.1.call-start = ((), (), s32[]{:S(2)}) async-start(), calls=%async_computation.10 | async-start | bytes 327680 | tf_op jit(solution)/shard_map/while/body/eval_jaxpr/reduce_scatter | solution.py:285
  1025.1 6.3 copy-start.16
  1028.7 43.4 %reduce-scatter.5.cloned.1.call-start = ((), (), s32[]{:S(2)}) async-start(), calls=%async_computation.11 | async-start | bytes 327680 | tf_op jit(solution)/shard_map/while/body/eval_jaxpr/reduce_scatter | solution.py:291
  1073.6 188.9 %all-reduce.7.cloned.1.call-start = ((), (), s32[]{:S(2)}) async-start(), calls=%async_computation.9 | async-start | bytes 16515072 | tf_op jit(solution)/shard_map/psum | solution.py:320
  (64 other events, 174.5 us)
Sparse Core Ops, SparseCore 0:
  19.2 100.2 all-gather.9
  121.1 16.6 all-gather.17
  139.8 179.7 all-gather.19
  321.7 26.6 all-gather.13
  350.4 22.5 all-gather.11
  374.9 58.5 all-gather.15
  435.6 152.2 all-gather.21
  615.1 18.1 reduce-scatter.2
  636.6 20.0 reduce-scatter.4
  672.7 19.9 reduce-scatter.2
  696.0 20.0 reduce-scatter.4
  732.1 20.0 reduce-scatter.2
  755.3 20.0 reduce-scatter.4
  791.5 19.9 reduce-scatter.2
  814.6 20.0 reduce-scatter.4
  850.8 19.9 reduce-scatter.2
  873.8 20.0 reduce-scatter.4
  910.0 19.9 reduce-scatter.2
  933.2 20.0 reduce-scatter.4
  969.4 19.9 reduce-scatter.2
  992.6 20.0 reduce-scatter.4
  1028.8 20.0 reduce-scatter.2
  1052.0 20.0 reduce-scatter.4
  1082.2 180.2 all-reduce.6
